TPU v7x, 256 devices: a whole 4x4x8 slice. The times are simulated.
256 devices in a mesh: wrap: 16 (over x, y_lo, core), normal: 16 (over y_hi, z).
Axes of the slice: x: 4, y: 4 (y_hi: 2, y_lo: 2; y = y_hi * 2 + y_lo), z: 8, core: 2. Of those that a mesh axis runs over, the one named last changes fastest.
Arguments:
- residual: float32 [5, 2, 1024, 2048], P(None, None, 'normal', 'wrap'), may hold values from -144 to 144
- courant_xi: float32 [5, 2, 1024, 2048], P(None, None, 'normal', 'wrap'), may hold values from -300 to 300
- courant_eta: float32 [5, 2, 1024, 2048], P(None, None, 'normal', 'wrap'), may hold values from -300 to 300
- dissip_xi: float32 [2, 1024, 2048], P(None, 'normal', 'wrap'), may hold values from 0.02 to 2
- dissip_eta: float32 [2, 1024, 2048], P(None, 'normal', 'wrap'), may hold values from 0.02 to 2
- coupling: bfloat16 [5, 5, 2, 1024, 2048], P(None, None, None, 'normal', 'wrap'), may hold values from -2.5 to 2.5
Outputs:
- update: float32 [5, 2, 1024, 2048], P(None, None, 'normal', 'wrap')
All inputs are finite; a program needn't handle non-finite values.
Results may differ from a plain program's by a relative error of at most 0.0003.
Values sent between devices are 32-bit elements; how exact they have to be, the bound alone decides.
A program may use at most 128 MiB of HBM per device.

v0:
```python
import functools

import jax
import jax.numpy as jnp
from jax import lax
from jax.experimental import pallas as pl
from jax.experimental.pallas import tpu as pltpu
from jax.sharding import PartitionSpec as P

LANES = 128
SUBS = 8


class Stash:
    def __init__(self, ref):
        self.ref, self.used = ref, 0

    def put(self, value):
        rows = value.shape[0]
        start = self.used
        self.used += -(-rows // 8) * 8
        assert self.used <= self.ref.shape[0]
        self.ref[pl.ds(start, rows), :] = value
        return lambda: self.ref[pl.ds(start, rows), :]

    def put_all(self, values):
        return [self.put(value) for value in values]


def fetch(handles):
    return [handle() for handle in handles]


def inverse2(m):
    scale = 1.0 / (m[0] * m[3] - m[1] * m[2])
    return [m[3] * scale, -(m[1] * scale), -(m[2] * scale), m[0] * scale]


def mm(a, b):
    return [
        a[0] * b[0] + a[1] * b[2],
        a[0] * b[1] + a[1] * b[3],
        a[2] * b[0] + a[3] * b[2],
        a[2] * b[1] + a[3] * b[3],
    ]


def mv(a, x):
    return [a[0] * x[0] + a[1] * x[1], a[2] * x[0] + a[3] * x[1]]


def sub(a, b):
    return [p - q for p, q in zip(a, b)]


def add(a, b):
    return [p + q for p, q in zip(a, b)]


def neg(a):
    return [-p for p in a]


def roll(values, shift):
    return [pltpu.roll(v, shift % v.shape[0], 0) for v in values]


def eliminate(cells, speed, damp, spread, source, keep_left, keep_right, stash, keep_rhs_factors):
    b = [damp(j) for j in range(cells)]
    c = [speed(j) for j in range(cells)]
    wide = [spread(v) for v in b]
    off = [spread(-2.0 * (b[j] + b[j + 1])) for j in range(cells - 1)]
    diag = [None] + [spread(1.0 + b[j - 1] + 4.0 * b[j] + b[j + 1]) for j in range(1, cells - 1)]
    diag.append(spread(1.0 + b[cells - 2] + 4.0 * b[cells - 1]))
    edge_l = wide[0] * keep_left
    edge_r = wide[-1] * keep_right
    diag.append(edge_r)
    skew = [0.25 * (c[j] + c[j + 1]) for j in range(cells - 1)]
    above = [off[j] + skew[j] for j in range(cells - 1)]
    below = [off[j] - skew[j] for j in range(cells - 1)]
    skew_l = 0.25 * c[0] * keep_left
    skew_r = 0.25 * c[-1] * keep_right
    above.append(-2.0 * edge_r + skew_r)
    below.append(-2.0 * edge_r - skew_r)
    ll = [edge_l, -2.0 * edge_l + skew_l, -2.0 * edge_l - skew_l, spread(1.0 + 4.0 * b[0] + b[1])]
    e, e_next = [edge_l, below[0]], [None, wide[1]]
    f, f_next = [edge_l, above[0]], [None, wide[1]]
    d, p, q, d_next = diag[1], above[1], below[1], diag[2]
    with_rhs = source is not None
    if with_rhs:
        r = [source(j) for j in range(cells)]
        r_left = [None, r[0]]
        here, after = r[1], r[2]
    saved = []
    for i in range(1, cells - 1):
        t = wide[i + 1] if i < cells - 2 else edge_r
        inv = 1.0 / d
        w1, w2 = inv * p, inv * t
        wl = [inv * e[0], inv * e[1]]
        keep = [w1, w2, wl[0], wl[1]]
        if with_rhs:
            wr = inv * here
            r_left = [-(f[0] * wr) if r_left[0] is None else r_left[0] - f[0] * wr, r_left[1] - f[1] * wr]
            tail = t * wr
            here, after = after - q * wr, (r[i + 2] - tail if i + 2 < cells else -tail)
            keep.append(wr)
        if keep_rhs_factors:
            keep += [inv, q, t, f[0], f[1]]
        saved.append(stash.put_all(keep))
        ll = [ll[0] - f[0] * wl[0], ll[1] - f[0] * wl[1], ll[2] - f[1] * wl[0], ll[3] - f[1] * wl[1]]
        e, e_next = (
            [-(q * wl[a]) if e_next[a] is None else e_next[a] - q * wl[a] for a in (0, 1)],
            [-(t * wl[a]) for a in (0, 1)],
        )
        f, f_next = (
            [-(f[a] * w1) if f_next[a] is None else f_next[a] - f[a] * w1 for a in (0, 1)],
            [-(f[a] * w2) for a in (0, 1)],
        )
        d, p, q, d_next = (
            d_next - q * w1,
            above[i + 1] - q * w2,
            below[i + 1] - t * w1,
            diag[i + 2] - t * w2,
        )
    matrix = ll + [f[0], f_next[0], f[1], f_next[1]] + [e[0], e[1], e_next[0], e_next[1]] + [d, p, q, d_next]
    rhs = r_left + [here, after] if with_rhs else None
    return matrix, rhs, saved


def forward_rhs(cells, source, saved, stash):
    r = [source(j) for j in range(cells)]
    r_left = [None, r[0]]
    here, after = r[1], r[2]
    kept = []
    for i in range(1, cells - 1):
        inv, q, t, f0, f1 = fetch(saved[i - 1][4:9])
        wr = inv * here
        kept.append(stash.put(wr))
        r_left = [-(f0 * wr) if r_left[0] is None else r_left[0] - f0 * wr, r_left[1] - f1 * wr]
        tail = t * wr
        here, after = after - q * wr, (r[i + 2] - tail if i + 2 < cells else -tail)
    return r_left + [here, after], kept


def back(cells, saved, results, joints, write):
    left, right = joints[:2], joints[2:]
    write(0, left[1])
    write(cells - 1, right[0])
    nearer, farther = right[0], right[1]
    for i in range(cells - 2, 0, -1):
        w1, w2, wl0, wl1 = fetch(saved[i - 1][:4])
        value = results[i - 1]() - wl0 * left[0] - wl1 * left[1] - w2 * farther - w1 * nearer
        write(i, value)
        nearer, farther = value, nearer


def merge_matrix(a, b):
    inv = inverse2(add(a[12:16], b[0:4]))
    lm, rm = a[4:8], b[8:12]
    wl, wr = mm(inv, a[8:12]), mm(inv, b[4:8])
    merged = (
        sub(a[0:4], mm(lm, wl)) + neg(mm(lm, wr)) + neg(mm(rm, wl)) + sub(b[12:16], mm(rm, wr))
    )
    return merged, wl + wr + inv + lm + rm


def merge_rhs(a, b, factors):
    inv, lm, rm = factors[8:12], factors[12:16], factors[16:20]
    w = mv(inv, add(a[2:4], b[0:2]))
    return sub(a[0:2], mv(lm, w)) + sub(b[2:4], mv(rm, w)), w


def tree_matrix(parts, stash):
    levels = []
    while len(parts) > 1:
        merged, kept = [], []
        for k in range(0, len(parts), 2):
            m, factors = merge_matrix(parts[k](), parts[k + 1]())
            merged.append(functools.partial(lambda v: v, m))
            kept.append(stash.put_all(factors))
        parts = merged
        levels.append(kept)
    return parts[0](), levels


def tree_rhs(parts, levels, stash):
    kept = []
    for level in levels:
        merged, saved = [], []
        for k, factors in enumerate(level):
            m, w = merge_rhs(parts[2 * k], parts[2 * k + 1], [None] * 8 + fetch(factors[8:20]))
            merged.append(m)
            saved.append(stash.put_all(w))
        parts = merged
        kept.append(saved)
    return parts[0], kept


def tree_back(joints, levels, results):
    spans = [joints]
    for level, saved in zip(reversed(levels), reversed(results)):
        finer = []
        for span, factors, w in zip(spans, level, saved):
            k = fetch(factors[:8])
            middle = sub(sub(fetch(w), mv(k[0:4], span[0:2])), mv(k[4:8], span[2:4]))
            finer.append(span[0:2] + middle)
            finer.append(middle + span[2:4])
        spans = finer
    return spans


def ring_matrix(even, odd, stash):
    before = roll(odd, 1)
    d_even, l_even, u_even = add(even[0:4], before[12:16]), before[8:12], even[4:8]
    d_odd, l_odd, u_odd = add(odd[0:4], even[12:16]), even[8:12], odd[4:8]
    inv = inverse2(d_odd)
    alpha, beta = mm(l_even, roll(inv, 1)), mm(u_even, inv)
    low = neg(mm(alpha, roll(l_odd, 1)))
    high = neg(mm(beta, u_odd))
    mid = sub(sub(d_even, mm(alpha, roll(u_odd, 1))), mm(beta, l_odd))
    factors = [alpha + beta]
    half = d_even[0].shape[0]
    step = 1
    while step < half:
        inv_mid = inverse2(mid)
        alpha = mm(low, roll(inv_mid, step))
        beta = mm(high, roll(inv_mid, -step))
        low_b, low_a = roll(low, step), roll(low, -step)
        high_b, high_a = roll(high, step), roll(high, -step)
        mid = sub(sub(mid, mm(alpha, high_b)), mm(beta, low_a))
        low, high = neg(mm(alpha, low_b)), neg(mm(beta, high_a))
        factors.append(alpha + beta)
        step *= 2
    last = inverse2(add(add(low, mid), high))
    kept = [stash.put_all(level) for level in factors]
    return kept, stash.put_all(last), stash.put_all(mm(inv, l_odd) + mm(inv, u_odd) + inv)


def ring_rhs(even, odd, ring):
    kept, last, outer = ring
    before = roll(odd[2:4], 1)
    f_even, f_odd = add(even[0:2], before), add(odd[0:2], even[2:4])
    k = fetch(kept[0])
    f = sub(sub(f_even, mv(k[0:4], roll(f_odd, 1))), mv(k[4:8], f_odd))
    step = 1
    for level in kept[1:]:
        k = fetch(level)
        f = sub(sub(f, mv(k[0:4], roll(f, step))), mv(k[4:8], roll(f, -step)))
        step *= 2
    x_even = mv(fetch(last), f)
    after = roll(x_even, -1)
    k = fetch(outer)
    x_odd = sub(sub(mv(k[8:12], f_odd), mv(k[0:4], x_even)), mv(k[4:8], after))
    return x_even + x_odd, x_odd + after


def kernel(
    fields, ring_w, ring_n, rows_n,
    residual_hbm, cxi_hbm, ceta_hbm, dxi_hbm, deta_hbm, coupling_hbm,
    out_ref,
    residual, cxi, ceta, dxi, deta, coupling,
    turned_c, turned_r, turned_b, mixed, small_xi, small_eta,
    send_xi, recv_xi, back_send_xi, back_recv_xi,
    send_m, recv_m, send_r, recv_r, back_send_eta, back_recv_eta,
    joints_xi, joints_eta, stash_cells, stash_small, stash_ring,
    in_sems, send_xi_sem, recv_xi_sem, bsend_xi_sem, brecv_xi_sem,
    send_m_sem, recv_m_sem, send_r_sem, recv_r_sem, bsend_eta_sem, brecv_eta_sem,
):
    me_w, me_n = lax.axis_index("wrap"), lax.axis_index("normal")
    lines = 2 * fields
    cells_w, cells_n = LANES // SUBS, rows_n // SUBS
    small = Stash(stash_small)
    cell_store = Stash(stash_cells)

    pairs = [(cxi_hbm, cxi), (dxi_hbm, dxi), (residual_hbm, residual), (ceta_hbm, ceta), (deta_hbm, deta), (coupling_hbm, coupling)]
    loads = [pltpu.make_async_copy(s, t, in_sems.at[i]) for i, (s, t) in enumerate(pairs)]
    for load in loads:
        load.start()

    barrier = pltpu.get_barrier_semaphore()

    def greet(axis, me, size):
        def one(o, carry):
            pl.semaphore_signal(barrier, inc=1, device_id={axis: lax.rem(me + o, size)}, device_id_type=pl.DeviceIdType.MESH)
            return carry

        lax.fori_loop(1, size, one, 0)

    greet("wrap", me_w, ring_w)
    greet("normal", me_n, ring_n)

    send_xi[...] = jnp.zeros_like(send_xi)
    send_r[...] = jnp.zeros_like(send_r)
    back_send_xi[...] = jnp.zeros_like(back_send_xi)
    back_send_eta[...] = jnp.zeros_like(back_send_eta)

    loads[0].wait()
    for f in range(fields):
        turned_c[pl.ds(f * LANES, LANES), :] = cxi[pl.ds(f * LANES, LANES), :].T
    loads[1].wait()
    turned_b[...] = dxi[...].T
    loads[2].wait()
    for f in range(fields):
        turned_r[pl.ds(f * LANES, LANES), :] = residual[pl.ds(f * LANES, LANES), :].T

    def every(ref, count, stride):
        return lambda j: ref[pl.ds(j, count, stride=stride), :]

    def tile(count):
        return lambda v: jnp.concatenate([v] * count, axis=0)

    rows_xi = fields * SUBS
    one_xi = jnp.float32(1.0)
    matrix, rhs, cells_xi = eliminate(
        cells_w, every(turned_c, rows_xi, cells_w), every(turned_b, SUBS, cells_w), tile(fields),
        every(turned_r, rows_xi, cells_w), one_xi, one_xi, cell_store, False,
    )
    for k, v in enumerate(matrix + rhs):
        small_xi[pl.ds(k * rows_xi, rows_xi), :] = v

    def packed(ref, rows, first, count):
        def part(g):
            return lambda: [ref[pl.ds(k * rows + first * SUBS + g, fields, stride=SUBS), :] for k in range(count)]

        return [part(g) for g in range(SUBS)]

    parts = packed(small_xi, rows_xi, 0, 16)
    whole, tree_xi = tree_matrix(parts, small)
    parts_r = [
        [small_xi[pl.ds(k * rows_xi + g, fields, stride=SUBS), :] for k in range(16, 20)] for g in range(SUBS)
    ]
    whole_r, tree_xi_r = tree_rhs(parts_r, tree_xi, small)
    for k, v in enumerate(whole + whole_r):
        send_xi[pl.ds(k, fields, stride=24), :] = v

    pl.semaphore_wait(barrier, ring_w + ring_n - 2)

    def remote(src, dst, send_sem, recv_sem, axis, target):
        return pltpu.make_async_remote_copy(
            src_ref=src, dst_ref=dst, send_sem=send_sem, recv_sem=recv_sem,
            device_id={axis: target}, device_id_type=pl.DeviceIdType.MESH,
        )

    def to_owner(count, size, rows, src, dst, send_sem, recv_sem, axis, me):
        copies = []
        for r in range(count):
            owner = size * r // count
            copy = remote(
                src.at[pl.ds(r * rows, rows), :], dst.at[pl.ds(pl.multiple_of(me * rows, rows), rows), :],
                send_sem.at[r], recv_sem.at[me], axis, owner,
            )

            @pl.when(me != owner)
            def _():
                copy.start()

            @pl.when(me == owner)
            def _():
                dst[pl.ds(owner * rows, rows), :] = src[pl.ds(r * rows, rows), :]

            copies.append((owner, copy))
        return copies

    def owned(count, size, me):
        r = lax.div(me * count + size - 1, size)
        return r, lax.div(r * size, count) == me

    def arrivals(size, rows, dst, recv_sem, axis, me):
        def one(o, carry):
            d = lax.rem(me + o, size)
            slot = dst.at[pl.ds(pl.multiple_of(d * rows, rows), rows), :]
            remote(slot, slot, recv_sem.at[d], recv_sem.at[d], axis, d).wait_recv()
            return carry

        lax.fori_loop(1, size, one, 0)

    def hand_back(r, size, answer, src, dst, send_sem, recv_sem, axis, me):
        for k in range(4):
            src[pl.ds(k, size // 2, stride=16), :] = answer[0][k]
            src[pl.ds(8 + k, size // 2, stride=16), :] = answer[1][k]
        into = dst.at[pl.ds(pl.multiple_of(r * 8, 8), 8), :]

        def one(o, carry):
            d = lax.rem(me + o, size)
            remote(src.at[pl.ds(pl.multiple_of(d * 8, 8), 8), :], into, send_sem.at[d], recv_sem.at[r], axis, d).start()
            return carry

        lax.fori_loop(1, size, one, 0)
        dst[pl.ds(pl.multiple_of(r * 8, 8), 8), :] = src[pl.ds(pl.multiple_of(me * 8, 8), 8), :]

    def wait_back(count, size, dst, recv_sem, axis, me):
        for r in range(count):
            owner = size * r // count
            slot = dst.at[pl.ds(r * 8, 8), :]

            @pl.when(me != owner)
            def _():
                remote(slot, slot, recv_sem.at[r], recv_sem.at[r], axis, owner).wait_recv()

    xi_copies = to_owner(fields, ring_w, 24, send_xi, recv_xi, send_xi_sem, recv_xi_sem, "wrap", me_w)

    loads[3].wait()
    loads[4].wait()
    rows_eta = lines * SUBS
    place = lax.rem(lax.broadcasted_iota(jnp.int32, (rows_eta, LANES), 0), SUBS)
    keep_left = jnp.where((place == 0) & (me_n == 0), 0.0, 1.0).astype(jnp.float32)
    keep_right = jnp.where((place == SUBS - 1) & (me_n == ring_n - 1), 0.0, 1.0).astype(jnp.float32)
    matrix, _, cells_eta = eliminate(
        cells_n, every(ceta, rows_eta, cells_n), every(deta, 2 * SUBS, cells_n), tile(fields),
        None, keep_left, keep_right, cell_store, True,
    )
    for k, v in enumerate(matrix):
        small_eta[pl.ds(k * rows_eta, rows_eta), :] = v

    r_xi, own_xi = owned(fields, ring_w, me_w)

    @pl.when(own_xi)
    def _():
        arrivals(ring_w, 24, recv_xi, recv_xi_sem, "wrap", me_w)
        even = [recv_xi[pl.ds(k, ring_w // 2, stride=48), :] for k in range(20)]
        odd = [recv_xi[pl.ds(24 + k, ring_w // 2, stride=48), :] for k in range(20)]
        ring = ring_matrix(even[:16], odd[:16], Stash(stash_ring))
        answer = ring_rhs(even[16:], odd[16:], ring)
        hand_back(r_xi, ring_w, answer, back_send_xi, back_recv_xi, bsend_xi_sem, brecv_xi_sem, "wrap", me_w)

    trees_eta = []
    for h in range(2):
        whole, tree = tree_matrix(packed(small_eta, rows_eta, h * fields, 16), small)
        for k, v in enumerate(whole):
            send_m[pl.ds(h * fields * 16 + k, fields, stride=16), :] = v
        trees_eta.append(tree)
    m_copies = to_owner(lines, ring_n, 16, send_m, recv_m, send_m_sem, recv_m_sem, "normal", me_n)

    def place_joints(spans, ref, rows, first):
        for g, span in enumerate(spans):
            for k in range(4):
                ref[pl.ds(k * rows + first * SUBS + g, fields, stride=SUBS), :] = span[k]

    wait_back(fields, ring_w, back_recv_xi, brecv_xi_sem, "wrap", me_w)
    joints = [back_recv_xi[pl.ds(k, fields, stride=8), :] for k in range(4)]
    place_joints(tree_back(joints, tree_xi, tree_xi_r), joints_xi, rows_xi, 0)

    def write_xi(j, value):
        turned_r[pl.ds(j, rows_xi, stride=cells_w), :] = value

    back(
        cells_w, cells_xi, [s[4] for s in cells_xi],
        [joints_xi[pl.ds(k * rows_xi, rows_xi), :] for k in range(4)], write_xi,
    )
    for f in range(fields):
        turned_c[pl.ds(f * LANES, LANES), :] = turned_r[pl.ds(f * LANES, LANES), :].T

    loads[5].wait()

    def mix(q, carry):
        start = pl.multiple_of(q * 16, 16)
        xi = [turned_c[pl.ds(j * LANES + start, 16), :] for j in range(fields)]
        for k in range(fields):
            total = None
            for j in range(fields):
                term = coupling[pl.ds((k * fields + j) * LANES + start, 16), :].astype(jnp.float32) * xi[j]
                total = term if total is None else total + term
            mixed[pl.ds(k * LANES + start, 16), :] = total
        return carry

    lax.fori_loop(0, LANES // 16, mix, 0)

    rhs, cells_eta_r = forward_rhs(cells_n, every(mixed, rows_eta, cells_n), cells_eta, cell_store)
    for k, v in enumerate(rhs):
        small_eta[pl.ds(k * rows_eta, rows_eta), :] = v
    trees_eta_r = []
    for h in range(2):
        parts_r = [part() for part in packed(small_eta, rows_eta, h * fields, 4)]
        whole_r, kept = tree_rhs(parts_r, trees_eta[h], small)
        for k, v in enumerate(whole_r):
            send_r[pl.ds(h * fields * 8 + k, fields, stride=8), :] = v
        trees_eta_r.append(kept)
    r_copies = to_owner(lines, ring_n, 8, send_r, recv_r, send_r_sem, recv_r_sem, "normal", me_n)

    r_eta, own_eta = owned(lines, ring_n, me_n)

    @pl.when(own_eta)
    def _():
        arrivals(ring_n, 16, recv_m, recv_m_sem, "normal", me_n)
        even = [recv_m[pl.ds(k, ring_n // 2, stride=32), :] for k in range(16)]
        odd = [recv_m[pl.ds(16 + k, ring_n // 2, stride=32), :] for k in range(16)]
        ring = ring_matrix(even, odd, Stash(stash_ring))
        arrivals(ring_n, 8, recv_r, recv_r_sem, "normal", me_n)
        even = [recv_r[pl.ds(k, ring_n // 2, stride=16), :] for k in range(4)]
        odd = [recv_r[pl.ds(8 + k, ring_n // 2, stride=16), :] for k in range(4)]
        answer = ring_rhs(even, odd, ring)
        hand_back(r_eta, ring_n, answer, back_send_eta, back_recv_eta, bsend_eta_sem, brecv_eta_sem, "normal", me_n)

    wait_back(lines, ring_n, back_recv_eta, brecv_eta_sem, "normal", me_n)
    for h in range(2):
        joints = [back_recv_eta[pl.ds(h * fields * 8 + k, fields, stride=8), :] for k in range(4)]
        place_joints(tree_back(joints, trees_eta[h], trees_eta_r[h]), joints_eta, rows_eta, h * fields)

    def write_eta(j, value):
        out_ref[pl.ds(j, rows_eta, stride=cells_n), :] = value

    back(
        cells_n, cells_eta, cells_eta_r,
        [joints_eta[pl.ds(k * rows_eta, rows_eta), :] for k in range(4)], write_eta,
    )

    for me, copies in ((me_w, xi_copies), (me_n, m_copies), (me_n, r_copies)):
        for owner, copy in copies:

            @pl.when(me != owner)
            def _():
                copy.wait_send()

    def drain(size, src, send_sem, axis, me):
        def one(o, carry):
            d = lax.rem(me + o, size)
            slot = src.at[pl.ds(pl.multiple_of(d * 8, 8), 8), :]
            remote(slot, slot, send_sem.at[d], send_sem.at[d], axis, d).wait_send()
            return carry

        lax.fori_loop(1, size, one, 0)

    @pl.when(own_xi)
    def _():
        drain(ring_w, back_send_xi, bsend_xi_sem, "wrap", me_w)

    @pl.when(own_eta)
    def _():
        drain(ring_n, back_send_eta, bsend_eta_sem, "normal", me_n)


def solution(mesh):
    ring_w, ring_n = mesh.shape["wrap"], mesh.shape["normal"]

    def local(residual, courant_xi, courant_eta, dissip_xi, dissip_eta, coupling):
        fields, _, rows_n, _ = residual.shape
        lines = 2 * fields
        flat = fields * LANES
        cells_w, cells_n = LANES // SUBS, rows_n // SUBS
        xi_rows, eta_rows = fields * SUBS, lines * SUBS
        pad = -(-fields // 8) * 8
        vmem = lambda rows, dtype=jnp.float32: pltpu.VMEM((rows, LANES), dtype)
        dma = lambda count: pltpu.SemaphoreType.DMA((count,))
        scratch = [
            vmem(flat), vmem(flat), vmem(flat), vmem(LANES), vmem(LANES), vmem(fields * flat, jnp.bfloat16),
            vmem(flat), vmem(flat), vmem(LANES), vmem(flat), vmem(20 * xi_rows), vmem(16 * eta_rows),
            vmem(fields * 24), vmem(ring_w * 24), vmem(ring_w * 8), vmem(fields * 8),
            vmem(lines * 16), vmem(ring_n * 16), vmem(lines * 8), vmem(ring_n * 8), vmem(ring_n * 8), vmem(lines * 8),
            vmem(4 * xi_rows), vmem(4 * eta_rows),
            vmem((cells_w - 2) * 5 * xi_rows + (cells_n - 2) * 10 * eta_rows),
            vmem((SUBS - 1) * 22 * 3 * pad),
            vmem((8 * 8 + 4 + 12) * max(8, ring_w // 2, ring_n // 2)),
            dma(6), dma(fields), dma(ring_w), dma(ring_w), dma(fields),
            dma(lines), dma(ring_n), dma(lines), dma(ring_n), dma(ring_n), dma(lines),
        ]
        out = pl.pallas_call(
            functools.partial(kernel, fields, ring_w, ring_n, rows_n),
            out_shape=jax.ShapeDtypeStruct((flat, LANES), jnp.float32),
            in_specs=[pl.BlockSpec(memory_space=pl.ANY)] * 6,
            out_specs=pl.BlockSpec(memory_space=pltpu.VMEM),
            scratch_shapes=scratch,
            compiler_params=pltpu.CompilerParams(
                collective_id=0, has_side_effects=True, vmem_limit_bytes=32 * 1024 * 1024
            ),
        )(
            residual.reshape(flat, LANES), courant_xi.reshape(flat, LANES), courant_eta.reshape(flat, LANES),
            dissip_xi.reshape(LANES, LANES), dissip_eta.reshape(LANES, LANES), coupling.reshape(fields * flat, LANES),
        )
        return out.reshape(residual.shape)

    placed = (
        P(None, None, "normal", "wrap"),
        P(None, None, "normal", "wrap"),
        P(None, None, "normal", "wrap"),
        P(None, "normal", "wrap"),
        P(None, "normal", "wrap"),
        P(None, None, None, "normal", "wrap"),
    )
    return jax.shard_map(
        local, mesh=mesh, in_specs=placed, out_specs=P(None, None, "normal", "wrap"), check_vma=False
    )
```

profile of v0, /device:TPU:6, one launch (start us, length us, event | category | flops | bytes accessed | tf_op | source)
XLA Modules:
  0.0 39.9 jit_solution(10177669410598409148)
XLA Ops:
  0.0 0.0 copy-start
  0.0 1.1 %copy-done = bf16[5,5,2,64,128]{4,3,2,1,0:T(8,128)(2,1)S(1)} copy-done((bf16[5,5,2,64,128]{4,3,2,1,0:T(8,128)(2,1)S(1)}, bf16[5,5,2,64,128]{4,3,2,1,0:T(8,128)(2,1)}, u32[]{:S(2)}) %copy-start) | copy-done | bytes 819224
  1.1 0.0 copy-start.1
  1.1 1.0 %copy-done.1 = f32[5,2,64,128]{3,2,1,0:T(8,128)S(1)} copy-done((f32[5,2,64,128]{3,2,1,0:T(8,128)S(1)}, f32[5,2,64,128]{3,2,1,0:T(8,128)}, u32[]{:S(2)}) %copy-start.1) | copy-done | bytes 327704
  2.1 0.0 copy-start.2
  2.1 1.0 %copy-done.2 = f32[5,2,64,128]{3,2,1,0:T(8,128)S(1)} copy-done((f32[5,2,64,128]{3,2,1,0:T(8,128)S(1)}, f32[5,2,64,128]{3,2,1,0:T(8,128)}, u32[]{:S(2)}) %copy-start.2) | copy-done | bytes 327704
  3.1 0.0 copy-start.3
  3.1 1.0 %copy-done.3 = f32[5,2,64,128]{3,2,1,0:T(8,128)S(1)} copy-done((f32[5,2,64,128]{3,2,1,0:T(8,128)S(1)}, f32[5,2,64,128]{3,2,1,0:T(8,128)}, u32[]{:S(2)}) %copy-start.3) | copy-done | bytes 327704
  4.1 0.0 copy-start.4
  4.1 0.8 %copy-done.4 = f32[2,64,128]{2,1,0:T(8,128)S(1)} copy-done((f32[2,64,128]{2,1,0:T(8,128)S(1)}, f32[2,64,128]{2,1,0:T(8,128)}, u32[]{:S(2)}) %copy-start.4) | copy-done | bytes 65560
  4.9 0.0 copy-start.5
  4.9 0.8 %copy-done.5 = f32[2,64,128]{2,1,0:T(8,128)S(1)} copy-done((f32[2,64,128]{2,1,0:T(8,128)S(1)}, f32[2,64,128]{2,1,0:T(8,128)}, u32[]{:S(2)}) %copy-start.5) | copy-done | bytes 65560
  5.7 33.4 %shard_map.64 = f32[640,128]{1,0:T(8,128)S(1)} custom-call(f32[640,128]{1,0:T(8,128)S(1)} %bitcast.9, f32[640,128]{1,0:T(8,128)S(1)} %bitcast.10, f32[640,128]{1,0:T(8,128)S(1)} %bitcast.11, f32[128,128]{1,0:T(8,128)S(1)} %bitcast.12, f32[128,128]{1,0:T(8,128)S(1)} %bitcast.13, bf16[3200,128]{1,0:T(8,128)(2,1)S(1)} %bitcast.8), custom_call_target="tpu_custom_call" | custom-call | tf_op jit(solution)/shard_map/pallas_call | solution.py:556
  39.2 0.7 %copy.8 = f32[5,2,64,128]{3,2,1,0:T(8,128)} copy(f32[5,2,64,128]{3,2,1,0:T(8,128)S(1)} %bitcast.7) | data formatting | bytes 655360
Async XLA Ops:
  0.0 1.1 %copy-start = (bf16[5,5,2,64,128]{4,3,2,1,0:T(8,128)(2,1)S(1)}, bf16[5,5,2,64,128]{4,3,2,1,0:T(8,128)(2,1)}, u32[]{:S(2)}) copy-start(bf16[5,5,2,64,128]{4,3,2,1,0:T(8,128)(2,1)} %param.11) | copy-start | bytes 2457604
  1.1 1.0 %copy-start.1 = (f32[5,2,64,128]{3,2,1,0:T(8,128)S(1)}, f32[5,2,64,128]{3,2,1,0:T(8,128)}, u32[]{:S(2)}) copy-start(f32[5,2,64,128]{3,2,1,0:T(8,128)} %param.6) | copy-start | bytes 983044
  2.1 1.0 %copy-start.2 = (f32[5,2,64,128]{3,2,1,0:T(8,128)S(1)}, f32[5,2,64,128]{3,2,1,0:T(8,128)}, u32[]{:S(2)}) copy-start(f32[5,2,64,128]{3,2,1,0:T(8,128)} %param.7) | copy-start | bytes 983044
  3.1 1.0 %copy-start.3 = (f32[5,2,64,128]{3,2,1,0:T(8,128)S(1)}, f32[5,2,64,128]{3,2,1,0:T(8,128)}, u32[]{:S(2)}) copy-start(f32[5,2,64,128]{3,2,1,0:T(8,128)} %param.8) | copy-start | bytes 983044
  4.1 0.8 %copy-start.4 = (f32[2,64,128]{2,1,0:T(8,128)S(1)}, f32[2,64,128]{2,1,0:T(8,128)}, u32[]{:S(2)}) copy-start(f32[2,64,128]{2,1,0:T(8,128)} %param.9) | copy-start | bytes 196612
  4.9 0.8 %copy-start.5 = (f32[2,64,128]{2,1,0:T(8,128)S(1)}, f32[2,64,128]{2,1,0:T(8,128)}, u32[]{:S(2)}) copy-start(f32[2,64,128]{2,1,0:T(8,128)} %param.10) | copy-start | bytes 196612
where the time goes:
time: 40.2 us; the launch traced here: 39.9 us
  Pallas kernels  33.4 us (83%)
  local copies, waits for them, and re-layouts  6.47 us (16%)
    pallas_call x1, Pallas kernels, local(): pl.pallas_call(functools.partial(kernel, fields, ring_w, ring_n, rows_n),...  33.4 us
    unnamed x13, local copies, waits for them, and re-layouts  6.47 us

commit v1 on v0

--- a/solution.py
+++ b/solution.py
@@ -556,15 +556,17 @@
         out = pl.pallas_call(
             functools.partial(kernel, fields, ring_w, ring_n, rows_n),
             out_shape=jax.ShapeDtypeStruct((flat, LANES), jnp.float32),
-            in_specs=[pl.BlockSpec(memory_space=pl.ANY)] * 6,
+            in_specs=[pl.BlockSpec(memory_space=pltpu.HBM)] * 6,
             out_specs=pl.BlockSpec(memory_space=pltpu.VMEM),
             scratch_shapes=scratch,
             compiler_params=pltpu.CompilerParams(
                 collective_id=0, has_side_effects=True, vmem_limit_bytes=32 * 1024 * 1024
             ),
         )(
+            *[pltpu.with_memory_space_constraint(v, pltpu.HBM) for v in (
             residual.reshape(flat, LANES), courant_xi.reshape(flat, LANES), courant_eta.reshape(flat, LANES),
             dissip_xi.reshape(LANES, LANES), dissip_eta.reshape(LANES, LANES), coupling.reshape(fields * flat, LANES),
+            )]
         )
         return out.reshape(residual.shape)
 

time: 40.2 us -> 33.6 us (0.84)
  local copies, waits for them, and re-layouts: 6.47 us -> 0.73 us
  Pallas kernels: 33.4 us -> 32.8 us
    unnamed x13 -> x1, local copies, waits for them, and re-layouts: 6.47 us -> 0.73 us
    pallas_call x1, Pallas kernels: 33.4 us -> 32.8 us  [local(): pl.pallas_call(functools.partial(kernel, fields, ring_w, ring_n, rows_n),...]
where the time goes in v1:
time: 33.6 us; the launch traced here: 33.5 us
  Pallas kernels  32.8 us (98%)
  local copies, waits for them, and re-layouts  0.73 us (2%)
    pallas_call x1, Pallas kernels, local(): pl.pallas_call(functools.partial(kernel, fields, ring_w, ring_n, rows_n),...  32.8 us
    unnamed x1, local copies, waits for them, and re-layouts  0.73 us

profile of v1, /device:TPU:6, one launch (start us, length us, event | category | flops | bytes accessed | tf_op | source)
XLA Modules:
  0.0 33.5 jit_solution(10335774860658787659)
XLA Ops:
  0.0 32.8 %shard_map.64 = f32[640,128]{1,0:T(8,128)S(1)} custom-call(f32[640,128]{1,0:T(8,128)} %bitcast.9, f32[640,128]{1,0:T(8,128)} %bitcast.10, f32[640,128]{1,0:T(8,128)} %bitcast.11, f32[128,128]{1,0:T(8,128)} %bitcast.12, f32[128,128]{1,0:T(8,128)} %bitcast.13, bf16[3200,128]{1,0:T(8,128)(2,1)} %bitcast.8), custom_call_target="tpu_custom_call" | custom-call | tf_op jit(solution)/shard_map/pallas_call | solution.py:556
  32.8 0.7 %copy.8 = f32[5,2,64,128]{3,2,1,0:T(8,128)} copy(f32[5,2,64,128]{3,2,1,0:T(8,128)S(1)} %bitcast.7) | data formatting | bytes 655360

commit v2 on v1

--- a/solution.py
+++ b/solution.py
@@ -209,6 +209,10 @@
     return spans
 
 
+def homes(lines, ring):
+    return ring // 2, [spot % (ring // 2) for spot in (0, 1, -1, 2, -2)[: lines // 2]]
+
+
 def ring_matrix(even, odd, stash):
     before = roll(odd, 1)
     d_even, l_even, u_even = add(even[0:4], before[12:16]), before[8:12], even[4:8]
@@ -290,9 +294,7 @@
     greet("normal", me_n, ring_n)
 
     send_xi[...] = jnp.zeros_like(send_xi)
-    send_r[...] = jnp.zeros_like(send_r)
     back_send_xi[...] = jnp.zeros_like(back_send_xi)
-    back_send_eta[...] = jnp.zeros_like(back_send_eta)
 
     loads[0].wait()
     for f in range(fields):
@@ -396,6 +398,40 @@
             @pl.when(me != owner)
             def _():
                 remote(slot, slot, recv_sem.at[r], recv_sem.at[r], axis, owner).wait_recv()
+
+    half, sites = homes(lines, ring_n)
+    my_half = lax.div(me_n, half)
+    my_spot = lax.rem(me_n, half)
+
+    def to_homes(rows, src, dst, send_sem, recv_sem):
+        size = 2 * rows
+        copies = []
+        for side in range(2):
+            for j, spot in enumerate(sites):
+                target = side * half + spot
+                begin = j * size
+                copy = remote(
+                    src.at[pl.ds(begin, size), :], dst.at[pl.ds(pl.multiple_of(me_n * size, size), size), :],
+                    send_sem.at[side * len(sites) + j], recv_sem.at[me_n], "normal", target,
+                )
+
+                @pl.when(me_n != target)
+                def _():
+                    copy.start()
+
+                @pl.when(me_n == target)
+                def _():
+                    dst[pl.ds(target * size, size), :] = src[pl.ds(begin, size), :]
+
+                copies.append((target, copy))
+        return copies
+
+    def home_copy(j, d):
+        return remote(
+            back_send_eta.at[pl.ds(pl.multiple_of(d * 8, 8), 8), :],
+            back_recv_eta.at[pl.ds(j * 8, 8), :],
+            bsend_eta_sem.at[lax.rem(d, half)], brecv_eta_sem.at[j], "normal", d,
+        )
 
     xi_copies = to_owner(fields, ring_w, 24, send_xi, recv_xi, send_xi_sem, recv_xi_sem, "wrap", me_w)
 
@@ -429,7 +465,7 @@
         for k, v in enumerate(whole):
             send_m[pl.ds(h * fields * 16 + k, fields, stride=16), :] = v
         trees_eta.append(tree)
-    m_copies = to_owner(lines, ring_n, 16, send_m, recv_m, send_m_sem, recv_m_sem, "normal", me_n)
+    m_copies = to_homes(16, send_m, recv_m, send_m_sem, recv_m_sem)
 
     def place_joints(spans, ref, rows, first):
         for g, span in enumerate(spans):
@@ -473,27 +509,57 @@
         parts_r = [part() for part in packed(small_eta, rows_eta, h * fields, 4)]
         whole_r, kept = tree_rhs(parts_r, trees_eta[h], small)
         for k, v in enumerate(whole_r):
-            send_r[pl.ds(h * fields * 8 + k, fields, stride=8), :] = v
+            send_r[pl.ds(h * fields * 4 + k, fields, stride=4), :] = v
         trees_eta_r.append(kept)
-    r_copies = to_owner(lines, ring_n, 8, send_r, recv_r, send_r_sem, recv_r_sem, "normal", me_n)
-
-    r_eta, own_eta = owned(lines, ring_n, me_n)
+    r_copies = to_homes(4, send_r, recv_r, send_r_sem, recv_r_sem)
+
+    own_eta = functools.reduce(lambda a, b: a | b, [my_spot == spot for spot in sites])
+
+    def each_home(act):
+        for j, spot in enumerate(sites):
+
+            @pl.when(my_spot == spot)
+            def _():
+                def one(o, carry):
+                    act(home_copy(j, my_half * half + lax.rem(spot + o, half)))
+                    return carry
+
+                lax.fori_loop(1, half, one, 0)
 
     @pl.when(own_eta)
     def _():
-        arrivals(ring_n, 16, recv_m, recv_m_sem, "normal", me_n)
-        even = [recv_m[pl.ds(k, ring_n // 2, stride=32), :] for k in range(16)]
-        odd = [recv_m[pl.ds(16 + k, ring_n // 2, stride=32), :] for k in range(16)]
-        ring = ring_matrix(even, odd, Stash(stash_ring))
+        arrivals(ring_n, 32, recv_m, recv_m_sem, "normal", me_n)
+        kept = Stash(stash_ring)
+
+        def by_parity(ref, i, rows, count):
+            slot = 2 * rows
+            return [
+                [ref[pl.ds(odd * slot + i * rows + k, ring_n // 2, stride=2 * slot), :] for k in range(count)]
+                for odd in range(2)
+            ]
+
+        rings = [ring_matrix(*by_parity(recv_m, i, 16, 16), kept) for i in range(2)]
         arrivals(ring_n, 8, recv_r, recv_r_sem, "normal", me_n)
-        even = [recv_r[pl.ds(k, ring_n // 2, stride=16), :] for k in range(4)]
-        odd = [recv_r[pl.ds(8 + k, ring_n // 2, stride=16), :] for k in range(4)]
-        answer = ring_rhs(even, odd, ring)
-        hand_back(r_eta, ring_n, answer, back_send_eta, back_recv_eta, bsend_eta_sem, brecv_eta_sem, "normal", me_n)
-
-    wait_back(lines, ring_n, back_recv_eta, brecv_eta_sem, "normal", me_n)
+        answers = [ring_rhs(*by_parity(recv_r, i, 4, 4), rings[i]) for i in range(2)]
+        for i, answer in enumerate(answers):
+            for k in range(4):
+                for odd in range(2):
+                    back_send_eta[pl.ds(odd * 8 + i * 4 + k, ring_n // 2, stride=16), :] = answer[odd][k]
+        each_home(lambda copy: copy.start())
+        for j, spot in enumerate(sites):
+
+            @pl.when(my_spot == spot)
+            def _():
+                back_recv_eta[pl.ds(j * 8, 8), :] = back_send_eta[pl.ds(pl.multiple_of(me_n * 8, 8), 8), :]
+
+    for j, spot in enumerate(sites):
+
+        @pl.when(my_spot != spot)
+        def _():
+            home_copy(j, my_half * half + spot).wait_recv()
+
     for h in range(2):
-        joints = [back_recv_eta[pl.ds(h * fields * 8 + k, fields, stride=8), :] for k in range(4)]
+        joints = [back_recv_eta[pl.ds(h * fields * 4 + k, fields, stride=4), :] for k in range(4)]
         place_joints(tree_back(joints, trees_eta[h], trees_eta_r[h]), joints_eta, rows_eta, h * fields)
 
     def write_eta(j, value):
@@ -526,7 +592,7 @@
 
     @pl.when(own_eta)
     def _():
-        drain(ring_n, back_send_eta, bsend_eta_sem, "normal", me_n)
+        each_home(lambda copy: copy.wait_send())
 
 
 def solution(mesh):
@@ -539,19 +605,20 @@
         cells_w, cells_n = LANES // SUBS, rows_n // SUBS
         xi_rows, eta_rows = fields * SUBS, lines * SUBS
         pad = -(-fields // 8) * 8
+        _, sites = homes(lines, ring_n)
         vmem = lambda rows, dtype=jnp.float32: pltpu.VMEM((rows, LANES), dtype)
         dma = lambda count: pltpu.SemaphoreType.DMA((count,))
         scratch = [
             vmem(flat), vmem(flat), vmem(flat), vmem(LANES), vmem(LANES), vmem(fields * flat, jnp.bfloat16),
             vmem(flat), vmem(flat), vmem(LANES), vmem(flat), vmem(20 * xi_rows), vmem(16 * eta_rows),
             vmem(fields * 24), vmem(ring_w * 24), vmem(ring_w * 8), vmem(fields * 8),
-            vmem(lines * 16), vmem(ring_n * 16), vmem(lines * 8), vmem(ring_n * 8), vmem(ring_n * 8), vmem(lines * 8),
+            vmem(lines * 16), vmem(ring_n * 32), vmem(lines * 4), vmem(ring_n * 8), vmem(ring_n * 8), vmem(lines * 4),
             vmem(4 * xi_rows), vmem(4 * eta_rows),
             vmem((cells_w - 2) * 5 * xi_rows + (cells_n - 2) * 10 * eta_rows),
             vmem((SUBS - 1) * 22 * 3 * pad),
-            vmem((8 * 8 + 4 + 12) * max(8, ring_w // 2, ring_n // 2)),
+            vmem(2 * (8 * 8 + 4 + 12) * max(8, ring_w // 2, ring_n // 2)),
             dma(6), dma(fields), dma(ring_w), dma(ring_w), dma(fields),
-            dma(lines), dma(ring_n), dma(lines), dma(ring_n), dma(ring_n), dma(lines),
+            dma(2 * len(sites)), dma(ring_n), dma(2 * len(sites)), dma(ring_n), dma(ring_n // 2), dma(len(sites)),
         ]
         out = pl.pallas_call(
             functools.partial(kernel, fields, ring_w, ring_n, rows_n),

time: 33.6 us -> 31 us (0.923)
  the two profiles are of different devices: /device:TPU:6 before, /device:TPU:32 now
where the time goes in v2:
time: 31 us; the launch traced here: 30.9 us
  Pallas kernels  30.2 us (97%)
  local copies, waits for them, and re-layouts  0.73 us (2%)
    pallas_call x1, Pallas kernels, local(): pl.pallas_call(functools.partial(kernel, fields, ring_w, ring_n, rows_n),...  30.2 us
    unnamed x1, local copies, waits for them, and re-layouts  0.73 us

profile of v2, /device:TPU:32, one launch (start us, length us, event | category | flops | bytes accessed | tf_op | source)
XLA Modules:
  0.0 30.9 jit_solution(12227132165937901876)
XLA Ops:
  0.0 30.2 %shard_map.64 = f32[640,128]{1,0:T(8,128)S(1)} custom-call(f32[640,128]{1,0:T(8,128)} %bitcast.9, f32[640,128]{1,0:T(8,128)} %bitcast.10, f32[640,128]{1,0:T(8,128)} %bitcast.11, f32[128,128]{1,0:T(8,128)} %bitcast.12, f32[128,128]{1,0:T(8,128)} %bitcast.13, bf16[3200,128]{1,0:T(8,128)(2,1)} %bitcast.8), custom_call_target="tpu_custom_call" | custom-call | tf_op jit(solution)/shard_map/pallas_call | solution.py:623
  30.2 0.7 %copy.8 = f32[5,2,64,128]{3,2,1,0:T(8,128)} copy(f32[5,2,64,128]{3,2,1,0:T(8,128)S(1)} %bitcast.7) | data formatting | bytes 655360

commit v3 on v2

--- a/solution.py
+++ b/solution.py
@@ -283,15 +283,28 @@
 
     barrier = pltpu.get_barrier_semaphore()
 
+    half, sites = homes(lines, ring_n)
+    my_half = lax.div(me_n, half)
+    my_spot = lax.rem(me_n, half)
+    own_eta = functools.reduce(lambda a, b: a | b, [my_spot == spot for spot in sites])
+    r_xi = lax.div(me_w * fields + ring_w - 1, ring_w)
+    own_xi = lax.div(r_xi * ring_w, fields) == me_w
+
     def greet(axis, me, size):
         def one(o, carry):
-            pl.semaphore_signal(barrier, inc=1, device_id={axis: lax.rem(me + o, size)}, device_id_type=pl.DeviceIdType.MESH)
+            d = o + (o >= me).astype(jnp.int32)
+            pl.semaphore_signal(barrier, inc=1, device_id={axis: d}, device_id_type=pl.DeviceIdType.MESH)
             return carry
 
-        lax.fori_loop(1, size, one, 0)
-
-    greet("wrap", me_w, ring_w)
-    greet("normal", me_n, ring_n)
+        lax.fori_loop(0, size - 1, one, 0)
+
+    @pl.when(own_eta)
+    def _():
+        greet("normal", me_n, ring_n)
+
+    @pl.when(own_xi)
+    def _():
+        greet("wrap", me_w, ring_w)
 
     send_xi[...] = jnp.zeros_like(send_xi)
     back_send_xi[...] = jnp.zeros_like(back_send_xi)
@@ -335,7 +348,8 @@
     for k, v in enumerate(whole + whole_r):
         send_xi[pl.ds(k, fields, stride=24), :] = v
 
-    pl.semaphore_wait(barrier, ring_w + ring_n - 2)
+    expected = fields - own_xi.astype(jnp.int32) + 2 * len(sites) - own_eta.astype(jnp.int32)
+    pl.semaphore_wait(barrier, expected)
 
     def remote(src, dst, send_sem, recv_sem, axis, target):
         return pltpu.make_async_remote_copy(
@@ -349,7 +363,7 @@
             owner = size * r // count
             copy = remote(
                 src.at[pl.ds(r * rows, rows), :], dst.at[pl.ds(pl.multiple_of(me * rows, rows), rows), :],
-                send_sem.at[r], recv_sem.at[me], axis, owner,
+                send_sem.at[r], recv_sem, axis, owner,
             )
 
             @pl.when(me != owner)
@@ -363,18 +377,9 @@
             copies.append((owner, copy))
         return copies
 
-    def owned(count, size, me):
-        r = lax.div(me * count + size - 1, size)
-        return r, lax.div(r * size, count) == me
-
-    def arrivals(size, rows, dst, recv_sem, axis, me):
-        def one(o, carry):
-            d = lax.rem(me + o, size)
-            slot = dst.at[pl.ds(pl.multiple_of(d * rows, rows), rows), :]
-            remote(slot, slot, recv_sem.at[d], recv_sem.at[d], axis, d).wait_recv()
-            return carry
-
-        lax.fori_loop(1, size, one, 0)
+    def await_rows(ref, rows, sem):
+        slot = ref.at[pl.ds(0, rows), :]
+        pltpu.make_async_copy(slot, slot, sem).wait()
 
     def hand_back(r, size, answer, src, dst, send_sem, recv_sem, axis, me):
         for k in range(4):
@@ -383,25 +388,22 @@
         into = dst.at[pl.ds(pl.multiple_of(r * 8, 8), 8), :]
 
         def one(o, carry):
-            d = lax.rem(me + o, size)
-            remote(src.at[pl.ds(pl.multiple_of(d * 8, 8), 8), :], into, send_sem.at[d], recv_sem.at[r], axis, d).start()
+            d = o + (o >= me).astype(jnp.int32)
+            remote(src.at[pl.ds(pl.multiple_of(d * 8, 8), 8), :], into, send_sem.at[d], recv_sem, axis, d).start()
             return carry
 
-        lax.fori_loop(1, size, one, 0)
+        lax.fori_loop(0, size - 1, one, 0)
         dst[pl.ds(pl.multiple_of(r * 8, 8), 8), :] = src[pl.ds(pl.multiple_of(me * 8, 8), 8), :]
 
-    def wait_back(count, size, dst, recv_sem, axis, me):
-        for r in range(count):
-            owner = size * r // count
-            slot = dst.at[pl.ds(r * 8, 8), :]
-
-            @pl.when(me != owner)
-            def _():
-                remote(slot, slot, recv_sem.at[r], recv_sem.at[r], axis, owner).wait_recv()
-
-    half, sites = homes(lines, ring_n)
-    my_half = lax.div(me_n, half)
-    my_spot = lax.rem(me_n, half)
+    def wait_back(rows, owner, ref, sem):
+        @pl.when(owner)
+        def _():
+            if rows > 8:
+                await_rows(ref, rows - 8, sem)
+
+        @pl.when(jnp.logical_not(owner))
+        def _():
+            await_rows(ref, rows, sem)
 
     def to_homes(rows, src, dst, send_sem, recv_sem):
         size = 2 * rows
@@ -412,7 +414,7 @@
                 begin = j * size
                 copy = remote(
                     src.at[pl.ds(begin, size), :], dst.at[pl.ds(pl.multiple_of(me_n * size, size), size), :],
-                    send_sem.at[side * len(sites) + j], recv_sem.at[me_n], "normal", target,
+                    send_sem.at[side * len(sites) + j], recv_sem, "normal", target,
                 )
 
                 @pl.when(me_n != target)
@@ -430,7 +432,7 @@
         return remote(
             back_send_eta.at[pl.ds(pl.multiple_of(d * 8, 8), 8), :],
             back_recv_eta.at[pl.ds(j * 8, 8), :],
-            bsend_eta_sem.at[lax.rem(d, half)], brecv_eta_sem.at[j], "normal", d,
+            bsend_eta_sem.at[lax.rem(d, half)], brecv_eta_sem, "normal", d,
         )
 
     xi_copies = to_owner(fields, ring_w, 24, send_xi, recv_xi, send_xi_sem, recv_xi_sem, "wrap", me_w)
@@ -448,11 +450,10 @@
     for k, v in enumerate(matrix):
         small_eta[pl.ds(k * rows_eta, rows_eta), :] = v
 
-    r_xi, own_xi = owned(fields, ring_w, me_w)
 
     @pl.when(own_xi)
     def _():
-        arrivals(ring_w, 24, recv_xi, recv_xi_sem, "wrap", me_w)
+        await_rows(recv_xi, (ring_w - 1) * 24, recv_xi_sem)
         even = [recv_xi[pl.ds(k, ring_w // 2, stride=48), :] for k in range(20)]
         odd = [recv_xi[pl.ds(24 + k, ring_w // 2, stride=48), :] for k in range(20)]
         ring = ring_matrix(even[:16], odd[:16], Stash(stash_ring))
@@ -467,12 +468,21 @@
         trees_eta.append(tree)
     m_copies = to_homes(16, send_m, recv_m, send_m_sem, recv_m_sem)
 
+    def all_sent(me, copies):
+        for owner, copy in copies:
+
+            @pl.when(me != owner)
+            def _():
+                copy.wait_send()
+
     def place_joints(spans, ref, rows, first):
         for g, span in enumerate(spans):
             for k in range(4):
                 ref[pl.ds(k * rows + first * SUBS + g, fields, stride=SUBS), :] = span[k]
 
-    wait_back(fields, ring_w, back_recv_xi, brecv_xi_sem, "wrap", me_w)
+    all_sent(me_w, xi_copies)
+
+    wait_back(fields * 8, own_xi, back_recv_xi, brecv_xi_sem)
     joints = [back_recv_xi[pl.ds(k, fields, stride=8), :] for k in range(4)]
     place_joints(tree_back(joints, tree_xi, tree_xi_r), joints_xi, rows_xi, 0)
 
@@ -512,8 +522,8 @@
             send_r[pl.ds(h * fields * 4 + k, fields, stride=4), :] = v
         trees_eta_r.append(kept)
     r_copies = to_homes(4, send_r, recv_r, send_r_sem, recv_r_sem)
-
-    own_eta = functools.reduce(lambda a, b: a | b, [my_spot == spot for spot in sites])
+    all_sent(me_n, m_copies)
+
 
     def each_home(act):
         for j, spot in enumerate(sites):
@@ -521,14 +531,14 @@
             @pl.when(my_spot == spot)
             def _():
                 def one(o, carry):
-                    act(home_copy(j, my_half * half + lax.rem(spot + o, half)))
+                    act(home_copy(j, my_half * half + o + (o >= spot).astype(jnp.int32)))
                     return carry
 
-                lax.fori_loop(1, half, one, 0)
+                lax.fori_loop(0, half - 1, one, 0)
 
     @pl.when(own_eta)
     def _():
-        arrivals(ring_n, 32, recv_m, recv_m_sem, "normal", me_n)
+        await_rows(recv_m, (ring_n - 1) * 32, recv_m_sem)
         kept = Stash(stash_ring)
 
         def by_parity(ref, i, rows, count):
@@ -539,7 +549,7 @@
             ]
 
         rings = [ring_matrix(*by_parity(recv_m, i, 16, 16), kept) for i in range(2)]
-        arrivals(ring_n, 8, recv_r, recv_r_sem, "normal", me_n)
+        await_rows(recv_r, (ring_n - 1) * 8, recv_r_sem)
         answers = [ring_rhs(*by_parity(recv_r, i, 4, 4), rings[i]) for i in range(2)]
         for i, answer in enumerate(answers):
             for k in range(4):
@@ -552,12 +562,8 @@
             def _():
                 back_recv_eta[pl.ds(j * 8, 8), :] = back_send_eta[pl.ds(pl.multiple_of(me_n * 8, 8), 8), :]
 
-    for j, spot in enumerate(sites):
-
-        @pl.when(my_spot != spot)
-        def _():
-            home_copy(j, my_half * half + spot).wait_recv()
-
+    all_sent(me_n, r_copies)
+    wait_back(lines * 4, own_eta, back_recv_eta, brecv_eta_sem)
     for h in range(2):
         joints = [back_recv_eta[pl.ds(h * fields * 4 + k, fields, stride=4), :] for k in range(4)]
         place_joints(tree_back(joints, trees_eta[h], trees_eta_r[h]), joints_eta, rows_eta, h * fields)
@@ -570,21 +576,14 @@
         [joints_eta[pl.ds(k * rows_eta, rows_eta), :] for k in range(4)], write_eta,
     )
 
-    for me, copies in ((me_w, xi_copies), (me_n, m_copies), (me_n, r_copies)):
-        for owner, copy in copies:
-
-            @pl.when(me != owner)
-            def _():
-                copy.wait_send()
-
     def drain(size, src, send_sem, axis, me):
         def one(o, carry):
-            d = lax.rem(me + o, size)
+            d = o + (o >= me).astype(jnp.int32)
             slot = src.at[pl.ds(pl.multiple_of(d * 8, 8), 8), :]
             remote(slot, slot, send_sem.at[d], send_sem.at[d], axis, d).wait_send()
             return carry
 
-        lax.fori_loop(1, size, one, 0)
+        lax.fori_loop(0, size - 1, one, 0)
 
     @pl.when(own_xi)
     def _():
@@ -617,8 +616,9 @@
             vmem((cells_w - 2) * 5 * xi_rows + (cells_n - 2) * 10 * eta_rows),
             vmem((SUBS - 1) * 22 * 3 * pad),
             vmem(2 * (8 * 8 + 4 + 12) * max(8, ring_w // 2, ring_n // 2)),
-            dma(6), dma(fields), dma(ring_w), dma(ring_w), dma(fields),
-            dma(2 * len(sites)), dma(ring_n), dma(2 * len(sites)), dma(ring_n), dma(ring_n // 2), dma(len(sites)),
+            dma(6), dma(fields), pltpu.SemaphoreType.DMA, dma(ring_w), pltpu.SemaphoreType.DMA,
+            dma(2 * len(sites)), pltpu.SemaphoreType.DMA, dma(2 * len(sites)), pltpu.SemaphoreType.DMA,
+            dma(ring_n // 2), pltpu.SemaphoreType.DMA,
         ]
         out = pl.pallas_call(
             functools.partial(kernel, fields, ring_w, ring_n, rows_n),

time: 31 us -> 30.4 us (0.981)
  Pallas kernels: 30.2 us -> 29.6 us
    pallas_call x1, Pallas kernels: 30.2 us -> 29.6 us  [local(): pl.pallas_call(functools.partial(kernel, fields, ring_w, ring_n, rows_n),...]
where the time goes in v3:
time: 30.4 us; the launch traced here: 30.3 us
  Pallas kernels  29.6 us (97%)
  local copies, waits for them, and re-layouts  0.73 us (2%)
    pallas_call x1, Pallas kernels, local(): pl.pallas_call(functools.partial(kernel, fields, ring_w, ring_n, rows_n),...  29.6 us
    unnamed x1, local copies, waits for them, and re-layouts  0.73 us

profile of v3, /device:TPU:32, one launch (start us, length us, event | category | flops | bytes accessed | tf_op | source)
XLA Modules:
  0.0 30.3 jit_solution(17180273710826793201)
XLA Ops:
  0.0 29.6 %shard_map.64 = f32[640,128]{1,0:T(8,128)S(1)} custom-call(f32[640,128]{1,0:T(8,128)} %bitcast.9, f32[640,128]{1,0:T(8,128)} %bitcast.10, f32[640,128]{1,0:T(8,128)} %bitcast.11, f32[128,128]{1,0:T(8,128)} %bitcast.12, f32[128,128]{1,0:T(8,128)} %bitcast.13, bf16[3200,128]{1,0:T(8,128)(2,1)} %bitcast.8), custom_call_target="tpu_custom_call" | custom-call | tf_op jit(solution)/shard_map/pallas_call | solution.py:623
  29.6 0.7 %copy.8 = f32[5,2,64,128]{3,2,1,0:T(8,128)} copy(f32[5,2,64,128]{3,2,1,0:T(8,128)S(1)} %bitcast.7) | data formatting | bytes 655360

commit v4 on v3

--- a/solution.py
+++ b/solution.py
@@ -278,7 +278,7 @@
 
     pairs = [(cxi_hbm, cxi), (dxi_hbm, dxi), (residual_hbm, residual), (ceta_hbm, ceta), (deta_hbm, deta), (coupling_hbm, coupling)]
     loads = [pltpu.make_async_copy(s, t, in_sems.at[i]) for i, (s, t) in enumerate(pairs)]
-    for load in loads:
+    for load in loads[:3]:
         load.start()
 
     barrier = pltpu.get_barrier_semaphore()
@@ -309,40 +309,57 @@
     send_xi[...] = jnp.zeros_like(send_xi)
     back_send_xi[...] = jnp.zeros_like(back_send_xi)
 
+    gap_w = cells_w + 1
+
+    def spaced(ref, f, value):
+        for g in range(SUBS):
+            ref[pl.ds((f * SUBS + g) * gap_w, cells_w), :] = value[g * cells_w : (g + 1) * cells_w]
+
     loads[0].wait()
     for f in range(fields):
-        turned_c[pl.ds(f * LANES, LANES), :] = cxi[pl.ds(f * LANES, LANES), :].T
+        spaced(turned_c, f, cxi[pl.ds(f * LANES, LANES), :].T)
     loads[1].wait()
-    turned_b[...] = dxi[...].T
+    spaced(turned_b, 0, dxi[...].T)
     loads[2].wait()
+    for load in loads[3:]:
+        load.start()
     for f in range(fields):
-        turned_r[pl.ds(f * LANES, LANES), :] = residual[pl.ds(f * LANES, LANES), :].T
+        spaced(turned_r, f, residual[pl.ds(f * LANES, LANES), :].T)
 
     def every(ref, count, stride):
         return lambda j: ref[pl.ds(j, count, stride=stride), :]
 
     def tile(count):
         return lambda v: jnp.concatenate([v] * count, axis=0)
+
+    gap = SUBS + 1
+
+    def put_parts(ref, k, rows, value):
+        for r in range(rows):
+            ref[pl.ds((k * rows + r) * gap, SUBS), :] = value[r * SUBS : (r + 1) * SUBS]
+
+    def get_parts(ref, k, rows):
+        return jnp.concatenate([ref[pl.ds((k * rows + r) * gap, SUBS), :] for r in range(rows)], axis=0)
 
     rows_xi = fields * SUBS
     one_xi = jnp.float32(1.0)
     matrix, rhs, cells_xi = eliminate(
-        cells_w, every(turned_c, rows_xi, cells_w), every(turned_b, SUBS, cells_w), tile(fields),
-        every(turned_r, rows_xi, cells_w), one_xi, one_xi, cell_store, False,
+        cells_w, every(turned_c, rows_xi, gap_w), every(turned_b, SUBS, gap_w), tile(fields),
+        every(turned_r, rows_xi, gap_w), one_xi, one_xi, cell_store, False,
     )
     for k, v in enumerate(matrix + rhs):
-        small_xi[pl.ds(k * rows_xi, rows_xi), :] = v
+        put_parts(small_xi, k, fields, v)
 
     def packed(ref, rows, first, count):
         def part(g):
-            return lambda: [ref[pl.ds(k * rows + first * SUBS + g, fields, stride=SUBS), :] for k in range(count)]
+            return lambda: [ref[pl.ds((k * rows + first) * gap + g, fields, stride=gap), :] for k in range(count)]
 
         return [part(g) for g in range(SUBS)]
 
-    parts = packed(small_xi, rows_xi, 0, 16)
+    parts = packed(small_xi, fields, 0, 16)
     whole, tree_xi = tree_matrix(parts, small)
     parts_r = [
-        [small_xi[pl.ds(k * rows_xi + g, fields, stride=SUBS), :] for k in range(16, 20)] for g in range(SUBS)
+        [small_xi[pl.ds(k * fields * gap + g, fields, stride=gap), :] for k in range(16, 20)] for g in range(SUBS)
     ]
     whole_r, tree_xi_r = tree_rhs(parts_r, tree_xi, small)
     for k, v in enumerate(whole + whole_r):
@@ -408,14 +425,19 @@
     def to_homes(rows, src, dst, send_sem, recv_sem):
         size = 2 * rows
         copies = []
-        for side in range(2):
+        for turn in range(2):
+            side = lax.rem(my_half + 1 + turn, 2)
             for j, spot in enumerate(sites):
                 target = side * half + spot
                 begin = j * size
                 copy = remote(
                     src.at[pl.ds(begin, size), :], dst.at[pl.ds(pl.multiple_of(me_n * size, size), size), :],
-                    send_sem.at[side * len(sites) + j], recv_sem, "normal", target,
+                    send_sem.at[turn * len(sites) + j], recv_sem, "normal", target,
                 )
+                copies.append((target, copy))
+                if turn == 0:
+                    copy.start()
+                    continue
 
                 @pl.when(me_n != target)
                 def _():
@@ -423,9 +445,8 @@
 
                 @pl.when(me_n == target)
                 def _():
-                    dst[pl.ds(target * size, size), :] = src[pl.ds(begin, size), :]
-
-                copies.append((target, copy))
+                    dst[pl.ds(pl.multiple_of(me_n * size, size), size), :] = src[pl.ds(begin, size), :]
+
         return copies
 
     def home_copy(j, d):
@@ -448,7 +469,7 @@
         None, keep_left, keep_right, cell_store, True,
     )
     for k, v in enumerate(matrix):
-        small_eta[pl.ds(k * rows_eta, rows_eta), :] = v
+        put_parts(small_eta, k, lines, v)
 
 
     @pl.when(own_xi)
@@ -462,7 +483,7 @@
 
     trees_eta = []
     for h in range(2):
-        whole, tree = tree_matrix(packed(small_eta, rows_eta, h * fields, 16), small)
+        whole, tree = tree_matrix(packed(small_eta, lines, h * fields, 16), small)
         for k, v in enumerate(whole):
             send_m[pl.ds(h * fields * 16 + k, fields, stride=16), :] = v
         trees_eta.append(tree)
@@ -478,23 +499,24 @@
     def place_joints(spans, ref, rows, first):
         for g, span in enumerate(spans):
             for k in range(4):
-                ref[pl.ds(k * rows + first * SUBS + g, fields, stride=SUBS), :] = span[k]
+                ref[pl.ds((k * rows + first) * gap + g, fields, stride=gap), :] = span[k]
 
     all_sent(me_w, xi_copies)
 
     wait_back(fields * 8, own_xi, back_recv_xi, brecv_xi_sem)
     joints = [back_recv_xi[pl.ds(k, fields, stride=8), :] for k in range(4)]
-    place_joints(tree_back(joints, tree_xi, tree_xi_r), joints_xi, rows_xi, 0)
+    place_joints(tree_back(joints, tree_xi, tree_xi_r), joints_xi, fields, 0)
 
     def write_xi(j, value):
-        turned_r[pl.ds(j, rows_xi, stride=cells_w), :] = value
+        turned_r[pl.ds(j, rows_xi, stride=gap_w), :] = value
 
     back(
         cells_w, cells_xi, [s[4] for s in cells_xi],
-        [joints_xi[pl.ds(k * rows_xi, rows_xi), :] for k in range(4)], write_xi,
+        [get_parts(joints_xi, k, fields) for k in range(4)], write_xi,
     )
     for f in range(fields):
-        turned_c[pl.ds(f * LANES, LANES), :] = turned_r[pl.ds(f * LANES, LANES), :].T
+        turned = [turned_r[pl.ds((f * SUBS + g) * gap_w, cells_w), :] for g in range(SUBS)]
+        turned_c[pl.ds(f * LANES, LANES), :] = jnp.concatenate(turned, axis=0).T
 
     loads[5].wait()
 
@@ -506,17 +528,20 @@
             for j in range(fields):
                 term = coupling[pl.ds((k * fields + j) * LANES + start, 16), :].astype(jnp.float32) * xi[j]
                 total = term if total is None else total + term
-            mixed[pl.ds(k * LANES + start, 16), :] = total
+            for half_rows in range(16 // cells_n):
+                mixed[pl.ds((k * LANES // cells_n + q * (16 // cells_n) + half_rows) * (cells_n + 1), cells_n), :] = (
+                    total[half_rows * cells_n : (half_rows + 1) * cells_n]
+                )
         return carry
 
     lax.fori_loop(0, LANES // 16, mix, 0)
 
-    rhs, cells_eta_r = forward_rhs(cells_n, every(mixed, rows_eta, cells_n), cells_eta, cell_store)
+    rhs, cells_eta_r = forward_rhs(cells_n, every(mixed, rows_eta, cells_n + 1), cells_eta, cell_store)
     for k, v in enumerate(rhs):
-        small_eta[pl.ds(k * rows_eta, rows_eta), :] = v
+        put_parts(small_eta, k, lines, v)
     trees_eta_r = []
     for h in range(2):
-        parts_r = [part() for part in packed(small_eta, rows_eta, h * fields, 4)]
+        parts_r = [part() for part in packed(small_eta, lines, h * fields, 4)]
         whole_r, kept = tree_rhs(parts_r, trees_eta[h], small)
         for k, v in enumerate(whole_r):
             send_r[pl.ds(h * fields * 4 + k, fields, stride=4), :] = v
@@ -566,14 +591,14 @@
     wait_back(lines * 4, own_eta, back_recv_eta, brecv_eta_sem)
     for h in range(2):
         joints = [back_recv_eta[pl.ds(h * fields * 4 + k, fields, stride=4), :] for k in range(4)]
-        place_joints(tree_back(joints, trees_eta[h], trees_eta_r[h]), joints_eta, rows_eta, h * fields)
+        place_joints(tree_back(joints, trees_eta[h], trees_eta_r[h]), joints_eta, lines, h * fields)
 
     def write_eta(j, value):
         out_ref[pl.ds(j, rows_eta, stride=cells_n), :] = value
 
     back(
         cells_n, cells_eta, cells_eta_r,
-        [joints_eta[pl.ds(k * rows_eta, rows_eta), :] for k in range(4)], write_eta,
+        [get_parts(joints_eta, k, lines) for k in range(4)], write_eta,
     )
 
     def drain(size, src, send_sem, axis, me):
@@ -609,10 +634,10 @@
         dma = lambda count: pltpu.SemaphoreType.DMA((count,))
         scratch = [
             vmem(flat), vmem(flat), vmem(flat), vmem(LANES), vmem(LANES), vmem(fields * flat, jnp.bfloat16),
-            vmem(flat), vmem(flat), vmem(LANES), vmem(flat), vmem(20 * xi_rows), vmem(16 * eta_rows),
+            vmem(flat + xi_rows), vmem(flat + xi_rows), vmem(LANES + SUBS), vmem(flat + eta_rows), vmem(20 * fields * (SUBS + 1)), vmem(16 * lines * (SUBS + 1)),
             vmem(fields * 24), vmem(ring_w * 24), vmem(ring_w * 8), vmem(fields * 8),
             vmem(lines * 16), vmem(ring_n * 32), vmem(lines * 4), vmem(ring_n * 8), vmem(ring_n * 8), vmem(lines * 4),
-            vmem(4 * xi_rows), vmem(4 * eta_rows),
+            vmem(4 * fields * (SUBS + 1)), vmem(4 * lines * (SUBS + 1)),
             vmem((cells_w - 2) * 5 * xi_rows + (cells_n - 2) * 10 * eta_rows),
             vmem((SUBS - 1) * 22 * 3 * pad),
             vmem(2 * (8 * 8 + 4 + 12) * max(8, ring_w // 2, ring_n // 2)),

time: 30.4 us -> 30.2 us (level)
  no operation moved by 1% of the time
where the time goes in v4:
time: 30.2 us; the launch traced here: 30.1 us
  Pallas kernels  29.3 us (97%)
  local copies, waits for them, and re-layouts  0.73 us (2%)
    pallas_call x1, Pallas kernels, local(): pl.pallas_call(functools.partial(kernel, fields, ring_w, ring_n, rows_n),...  29.3 us
    unnamed x1, local copies, waits for them, and re-layouts  0.73 us

profile of v4, /device:TPU:32, one launch (start us, length us, event | category | flops | bytes accessed | tf_op | source)
XLA Modules:
  0.0 30.1 jit_solution(9682611692512674446)
XLA Ops:
  0.0 29.3 %shard_map.64 = f32[640,128]{1,0:T(8,128)S(1)} custom-call(f32[640,128]{1,0:T(8,128)} %bitcast.9, f32[640,128]{1,0:T(8,128)} %bitcast.10, f32[640,128]{1,0:T(8,128)} %bitcast.11, f32[128,128]{1,0:T(8,128)} %bitcast.12, f32[128,128]{1,0:T(8,128)} %bitcast.13, bf16[3200,128]{1,0:T(8,128)(2,1)} %bitcast.8), custom_call_target="tpu_custom_call" | custom-call | tf_op jit(solution)/shard_map/pallas_call | solution.py:648
  29.3 0.7 %copy.8 = f32[5,2,64,128]{3,2,1,0:T(8,128)} copy(f32[5,2,64,128]{3,2,1,0:T(8,128)S(1)} %bitcast.7) | data formatting | bytes 655360

commit v5 on v4

--- a/solution.py
+++ b/solution.py
@@ -534,7 +534,7 @@
                 )
         return carry
 
-    lax.fori_loop(0, LANES // 16, mix, 0)
+    lax.fori_loop(0, LANES // 16, mix, 0, unroll=True)
 
     rhs, cells_eta_r = forward_rhs(cells_n, every(mixed, rows_eta, cells_n + 1), cells_eta, cell_store)
     for k, v in enumerate(rhs):

time: 30.2 us -> 30.1 us (level)
  no operation moved by 1% of the time
where the time goes in v5:
time: 30.1 us; the launch traced here: 30 us
  Pallas kernels  29.2 us (97%)
  local copies, waits for them, and re-layouts  0.73 us (2%)
    pallas_call x1, Pallas kernels, local(): pl.pallas_call(functools.partial(kernel, fields, ring_w, ring_n, rows_n),...  29.2 us
    unnamed x1, local copies, waits for them, and re-layouts  0.73 us

profile of v5, /device:TPU:32, one launch (start us, length us, event | category | flops | bytes accessed | tf_op | source)
XLA Modules:
  0.0 30.0 jit_solution(1382450873540898849)
XLA Ops:
  0.0 29.2 %shard_map.64 = f32[640,128]{1,0:T(8,128)S(1)} custom-call(f32[640,128]{1,0:T(8,128)} %bitcast.9, f32[640,128]{1,0:T(8,128)} %bitcast.10, f32[640,128]{1,0:T(8,128)} %bitcast.11, f32[128,128]{1,0:T(8,128)} %bitcast.12, f32[128,128]{1,0:T(8,128)} %bitcast.13, bf16[3200,128]{1,0:T(8,128)(2,1)} %bitcast.8), custom_call_target="tpu_custom_call" | custom-call | tf_op jit(solution)/shard_map/pallas_call | solution.py:648
  29.2 0.7 %copy.8 = f32[5,2,64,128]{3,2,1,0:T(8,128)} copy(f32[5,2,64,128]{3,2,1,0:T(8,128)S(1)} %bitcast.7) | data formatting | bytes 655360
